TPU v7x, 256 devices: a whole 4x4x8 slice. The times are simulated.
256 devices in a mesh: ctx: 32 (over x_lo, z, core), head: 8 (over x_hi, y).
Axes of the slice: x: 4 (x_hi: 2, x_lo: 2; x = x_hi * 2 + x_lo), y: 4, z: 8, core: 2. Of those that a mesh axis runs over, the one named last changes fastest.
Arguments:
- tokens: bfloat16 [8192, 3072], P('ctx', 'head'), may hold values from -48 to 48
- block_order: int32 [64], replicated, may hold values from 0 to 63, each once
- block_mask: int32 [64, 64], replicated, may hold values from 0 to 1, as said below
- w_query: bfloat16 [3072, 3072], P(None, 'head'), may hold values from -0.109375 to 0.109375
- w_key: bfloat16 [3072, 3072], P(None, 'head'), may hold values from -0.109375 to 0.109375
- w_value: bfloat16 [3072, 3072], P(None, 'head'), may hold values from -0.109375 to 0.109375
- w_out: bfloat16 [3072, 3072], P('head'), may hold values from -0.109375 to 0.109375
Outputs:
- mixed: bfloat16 [8192, 3072], P('ctx', 'head')
Inputs may be any that keep to these rules, and one draw needn't show every extreme that they name: `block_order`: a permutation of the block numbers. block_mask[f, f] = 1 for every block f.
All inputs are finite; a program needn't handle non-finite values.
Results may differ from a plain program's by a relative error of at most 0.02.
The roundings to bfloat16 on the way count: a program that leaves them out, or rounds other values in their place, can miss the bound.
Values may be sent and summed in bfloat16 or wider, within the bound.
A program may use at most 128 MiB of HBM per device.

v0:
```python
import jax
import jax.numpy as jnp
from jax import lax
from jax.sharding import PartitionSpec as P

HEAD_DIM = 128
BLOCK = 128


def per_device(tokens, block_order, block_mask, w_query, w_key, w_value, w_out):
    row_count = tokens.shape[0]
    local_width = w_query.shape[1]
    local_heads = local_width // HEAD_DIM
    block_count = block_order.shape[0]
    portion = lax.all_gather(tokens, "head", axis=1, tiled=True)
    projected = tuple(
        (
            jnp.dot(portion, weight, preferred_element_type=jnp.float32)
            for weight in (w_query, w_key, w_value)
        )
    )
    query_rows, key_rows, value_rows = [
        part_sum.astype(jnp.bfloat16).reshape(row_count, local_heads, HEAD_DIM)
        for part_sum in projected
    ]
    frame_ids = jnp.arange(block_count, dtype=jnp.int32)
    placed = (block_order[None, :] == frame_ids[:, None]).astype(jnp.float32)
    mask_float = block_mask.astype(jnp.float32)
    cycle_live = jnp.dot(
        jnp.dot(placed.T, mask_float, precision=lax.Precision.HIGHEST),
        placed,
        precision=lax.Precision.HIGHEST,
    )
    cycle_index = lax.axis_index("ctx")
    global_rows = cycle_index * row_count + jnp.arange(row_count, dtype=jnp.int32)
    row_blocks = global_rows // BLOCK
    row_pick = (row_blocks[:, None] == frame_ids[None, :]).astype(jnp.float32)
    live_columns = jnp.dot(row_pick, cycle_live, precision=lax.Precision.HIGHEST).T
    inv_root = 1.0 / HEAD_DIM**0.5

    def update(state, key_tile, value_tile, key_keep):
        top_now, total_now, accum = state
        scores = (
            jnp.einsum("qhd,khd->hqk", query_rows, key_tile, preferred_element_type=jnp.float32)
            * inv_root
        )
        allowed = key_keep[None, :, None]
        top_next = jnp.maximum(top_now, jnp.max(jnp.where(allowed, scores, -1e30), axis=-1))
        factor = jnp.exp(top_now - top_next)
        weights = jnp.where(allowed, jnp.exp(scores - top_next[..., None]), 0.0)
        total_next = total_now * factor + jnp.sum(weights, axis=-1)
        accum = accum * factor[..., None] + jnp.einsum(
            "hqk,khd->hqd",
            weights.astype(jnp.bfloat16),
            value_tile,
            preferred_element_type=jnp.float32,
        )
        return (top_next, total_next, accum)

    initial = (
        jnp.full((local_heads, row_count), -1e30, jnp.float32),
        jnp.zeros((local_heads, row_count), jnp.float32),
        jnp.zeros((local_heads, row_count, HEAD_DIM), jnp.float32),
    )
    carry = initial
    key_part = lax.all_gather(key_rows, "ctx", axis=0, tiled=True)
    value_part = lax.all_gather(value_rows, "ctx", axis=0, tiled=True)
    tile_count = key_part.shape[0] // BLOCK
    key_tiles = key_part.reshape(tile_count, BLOCK, local_heads, HEAD_DIM)
    value_tiles = value_part.reshape(tile_count, BLOCK, local_heads, HEAD_DIM)

    def advance(state, inputs):
        key_tile, value_tile, offset = inputs
        key_keep = lax.dynamic_index_in_dim(live_columns, offset, 0, keepdims=False) > 0.5
        state = update(state, key_tile, value_tile, key_keep)
        return (state, None)

    carry, _ = lax.scan(
        advance, carry, (key_tiles, value_tiles, jnp.arange(tile_count, dtype=jnp.int32))
    )
    top_final, total_final, accum_final = carry
    attended = (
        (accum_final / total_final[..., None])
        .transpose(1, 0, 2)
        .reshape(row_count, local_width)
        .astype(jnp.bfloat16)
    )
    partial_out = jnp.dot(attended, w_out, preferred_element_type=jnp.float32)
    return lax.psum_scatter(
        partial_out.astype(jnp.bfloat16), "head", scatter_dimension=1, tiled=True
    )


def solution(mesh):
    in_specs = (
        P("ctx", "head"),
        P(),
        P(),
        P(None, "head"),
        P(None, "head"),
        P(None, "head"),
        P("head", None),
    )
    out_specs = P("ctx", "head")
    return jax.shard_map(
        per_device, mesh=mesh, in_specs=in_specs, out_specs=out_specs, check_vma=False
    )
```

profile of v0, /device:TPU:32, one launch (start us, length us, event | category | flops | bytes accessed | tf_op | source)
XLA Modules:
  0.0 652.0 jit_solution(12298507190897239615)
XLA Ops:
  7.3 59.7 %all-gather.4.cloned.1.call-done = bf16[256,3072]{1,0:T(8,128)(2,1)} async-done(((bf16[256,384]{1,0:T(8,128)(2,1)}), bf16[256,3072]{1,0:T(8,128)(2,1)}) %all-gather.4.cloned.1.call-update) | async-done | bytes 1572880 | tf_op jit(solution)/shard_map/all_gather | solution.py:15
  67.0 3.1 convolution_convert_fusion.1
  71.1 3.1 convolution_convert_fusion.3
  75.8 3.1 convolution_convert_fusion.2
  79.3 69.0 %all-gather.8.cloned.1.call-done = bf16[8192,3,128]{0,2,1:T(8,128)(2,1)} async-done(((bf16[256,3,128]{0,2,1:T(8,128)(2,1)}), bf16[8192,3,128]{0,2,1:T(8,128)(2,1)}) %all-gather.8.cloned.1.call-update) | async-done | bytes 6291472 | tf_op jit(solution)/shard_map/all_gather | solution.py:67
  148.3 8.6 %copy.25 = bf16[8192,3,128]{2,0,1:T(8,128)(2,1)} copy(bf16[8192,3,128]{0,2,1:T(8,128)(2,1)} %all-gather.8.cloned.1.call-done) | data formatting | bytes 12582912 | tf_op jit(solution)/shard_map/all_gather | solution.py:67
  156.9 71.3 %all-gather.6.cloned.1.call-done = bf16[8192,3,128]{0,2,1:T(8,128)(2,1)} async-done(((bf16[256,3,128]{0,2,1:T(8,128)(2,1)}), bf16[8192,3,128]{0,2,1:T(8,128)(2,1)}) %all-gather.6.cloned.1.call-update) | async-done | bytes 6291472 | tf_op jit(solution)/shard_map/all_gather | solution.py:66
  228.2 8.6 %copy.22 = bf16[8192,3,128]{2,0,1:T(8,128)(2,1)} copy(bf16[8192,3,128]{0,2,1:T(8,128)(2,1)} %all-gather.6.cloned.1.call-done) | data formatting | bytes 12582912 | tf_op jit(solution)/shard_map/all_gather | solution.py:66
  236.8 323.9 %while.15 = (s32[]{:T(128)}, f32[3,256]{1,0:T(4,128)S(1)}, f32[3,256]{1,0:T(4,128)S(1)}, f32[3,256,128]{2,1,0:T(8,128)S(1)}, s32[64]{0:T(128)S(1)}, /*index=5*/f...) while((s32[]{:T(128)}, f32[3,256]{1,0:T(4,128)S(1)}, ...), condition=%wide.region_3.4_spmd.clone, body=%wide.region_0.3_spmd.clone.sunk | while | flops 51515396 | bytes 2410691 | solution.py:78
  250.7 1.2 convolution_add_fusion.2
  260.8 1.2 convolution_add_fusion.2
  265.9 1.2 convolution_add_fusion.2
  276.0 1.2 convolution_add_fusion.2
  281.1 1.2 convolution_add_fusion.2
  291.2 1.2 convolution_add_fusion.2
  301.3 1.2 convolution_add_fusion.2
  306.4 1.2 convolution_add_fusion.2
  316.5 1.2 convolution_add_fusion.2
  321.6 1.2 convolution_add_fusion.2
  331.7 1.2 convolution_add_fusion.2
  341.8 1.2 convolution_add_fusion.2
  346.9 1.2 convolution_add_fusion.2
  357.0 1.2 convolution_add_fusion.2
  362.1 1.2 convolution_add_fusion.2
  372.2 1.2 convolution_add_fusion.2
  377.2 1.2 convolution_add_fusion.2
  387.4 1.2 convolution_add_fusion.2
  397.5 1.2 convolution_add_fusion.2
  560.9 2.2 convolution_convert_fusion
  563.1 2.6 copy.31
  565.7 78.1 %reduce-scatter.4.cloned.1.call-done = bf16[384,256]{1,0:T(8,128)(2,1)} async-done(((bf16[3072,256]{1,0:T(8,128)(2,1)}), bf16[384,256]{1,0:T(8,128)(2,1)}) %reduce-scatter.4.cloned.1.call-update) | async-done | bytes 196624
  643.8 1.7 copy.32
  (521 shorter events, 177.1 us)
Async XLA Ops:
  6.5 554.4 %copy-start = (bf16[384,3072]{1,0:T(8,128)(2,1)S(1)}, bf16[384,3072]{1,0:T(8,128)(2,1)}, u32[]{:S(2)}) copy-start(bf16[384,3072]{1,0:T(8,128)(2,1)} %param.15) | copy-start | bytes 7077892
  6.5 60.5 %all-gather.4.cloned.1.call-start = ((), (), s32[]{:S(2)}) async-start(), calls=%async_computation.1 | async-start | bytes 1769472 | tf_op jit(solution)/shard_map/all_gather | solution.py:15
  7.3 141.0 %all-gather.8.cloned.1.call-start = ((), (), s32[]{:S(2)}) async-start(), calls=%async_computation.3 | async-start | bytes 6488064 | tf_op jit(solution)/shard_map/all_gather | solution.py:67
  71.0 4.2 copy-start.1
  71.0 4.2 copy-start.2
  71.0 157.2 %all-gather.6.cloned.1.call-start = ((), (), s32[]{:S(2)}) async-start(), calls=%async_computation.2 | async-start | bytes 6488064 | tf_op jit(solution)/shard_map/all_gather | solution.py:66
  75.0 568.7 %reduce-scatter.4.cloned.1.call-start = ((), (), s32[]{:S(2)}) async-start(), calls=%async_computation.4 | async-start | bytes 1769472
Sparse Core Ops, SparseCore 0:
  9.8 57.1 all-gather.3
  71.1 77.1 all-gather.7
  150.1 78.0 all-gather.5
  565.8 77.9 reduce-scatter.3
where the time goes:
time: 658 us; the launch traced here: 652 us
  waiting for transfers between devices  279 us (42%)
  matrix products  162 us (25%)
  loops' own time  127 us (19%)
  local copies, waits for them, and re-layouts  61.4 us (9%)
  between operations  13.3 us (2%)
  other arithmetic  8.91 us (1%)
    another operation x1, loops' own time, per_device(): lax.scan(advance, carry, (key_tiles, value_tiles, jnp.arange(tile_count,...  127 us
    unnamed x5, waiting for transfers between devices  78.9 us
    dot_general x64, matrix products, update(): jnp.einsum('hqk,khd->hqd', weights.astype(jnp.bfloat16), value_tile, pref...  77.5 us
    dot_general x64, matrix products, update(): jnp.einsum('qhd,khd->hqk', query_rows, key_tile, preferred_element_type=j...  72.4 us
    all_gather x1, waiting for transfers between devices, per_device(): key_part = lax.all_gather(key_rows, 'ctx', axis=0, tiled=True)  71.3 us
    all_gather x1, waiting for transfers between devices, per_device(): value_part = lax.all_gather(value_rows, 'ctx', axis=0, tiled=True)  69 us
    all_gather x1, waiting for transfers between devices, per_device(): portion = lax.all_gather(tokens, 'head', axis=1, tiled=True)  59.7 us
    dynamic_slice x64, local copies, waits for them, and re-layouts, per_device(): lax.scan(advance, carry, (key_tiles, value_tiles, jnp.arange(tile_count,...  37.5 us
  transfers between devices with their start and end apart: 4, of which 4 were waited for; matrix products, arithmetic and copies ran while one was open for 3% of the time, Pallas kernels for 0%

commit v1 on v0

--- a/solution.py
+++ b/solution.py
@@ -7,12 +7,17 @@
 BLOCK = 128
 
 
+def shape_quarters(local_array, axis_id):
+    value_now = jnp.stack([local_array for _ in range(lax.axis_size(axis_id))], axis=0)
+    return jnp.concatenate(lax.all_to_all(value_now, axis_id, 0, 0), axis=1)
+
+
 def per_device(tokens, block_order, block_mask, w_query, w_key, w_value, w_out):
     row_count = tokens.shape[0]
     local_width = w_query.shape[1]
     local_heads = local_width // HEAD_DIM
     block_count = block_order.shape[0]
-    portion = lax.all_gather(tokens, "head", axis=1, tiled=True)
+    portion = shape_quarters(tokens, "head")
     projected = tuple(
         (
             jnp.dot(portion, weight, preferred_element_type=jnp.float32)

time: 658 us -> 628 us (0.954)
  waiting for transfers between devices: 279 us -> 219 us
  blocking collectives: 0 us -> 29.6 us
    all_gather x1 -> x0, waiting for transfers between devices: 59.7 us -> none  [per_device(): portion = lax.all_gather(tokens, 'head', axis=1, tiled=True)]
    all_to_all x0 -> x1, blocking collectives: none -> 29.6 us  [shape_quarters(): return jnp.concatenate(lax.all_to_all(value_now, axis_id, 0, 0), axis=1)]
    unnamed x5 -> x4, waiting for transfers between devices: 78.9 us -> 78.2 us
  transfers between devices with their start and end apart: 4 -> 3, of which waited for: 4 -> 3; matrix products, arithmetic and copies ran while one was open for 3% -> 3% of each run, Pallas kernels for 0% -> 0%
where the time goes in v1:
time: 628 us; the launch traced here: 622 us
  waiting for transfers between devices  219 us (35%)
  matrix products  160 us (25%)
  loops' own time  127 us (20%)
  local copies, waits for them, and re-layouts  63.9 us (10%)
  blocking collectives  29.6 us (5%)
  between operations  13.3 us (2%)
  other arithmetic  8.91 us (1%)
    another operation x1, loops' own time, per_device(): lax.scan(advance, carry, (key_tiles, value_tiles, jnp.arange(tile_count,...  127 us
    unnamed x4, waiting for transfers between devices  78.2 us
    dot_general x64, matrix products, update(): jnp.einsum('hqk,khd->hqd', weights.astype(jnp.bfloat16), value_tile, pref...  77.5 us
    dot_general x64, matrix products, update(): jnp.einsum('qhd,khd->hqk', query_rows, key_tile, preferred_element_type=j...  72.4 us
    all_gather x1, waiting for transfers between devices, per_device(): key_part = lax.all_gather(key_rows, 'ctx', axis=0, tiled=True)  71.2 us
    all_gather x1, waiting for transfers between devices, per_device(): value_part = lax.all_gather(value_rows, 'ctx', axis=0, tiled=True)  69.6 us
    dynamic_slice x64, local copies, waits for them, and re-layouts, per_device(): lax.scan(advance, carry, (key_tiles, value_tiles, jnp.arange(tile_count,...  37.5 us
    all_to_all x1, blocking collectives, shape_quarters(): return jnp.concatenate(lax.all_to_all(value_now, axis_id, 0, 0), axis=1)  29.6 us
  transfers between devices with their start and end apart: 3, of which 3 were waited for; matrix products, arithmetic and copies ran while one was open for 3% of the time, Pallas kernels for 0%

profile of v1, /device:TPU:32, one launch (start us, length us, event | category | flops | bytes accessed | tf_op | source)
XLA Modules:
  0.0 622.2 jit_solution(4880684858560692670)
XLA Ops:
  7.9 29.6 %all_to_all.5 = bf16[8,256,384]{1,2,0:T(8,128)(2,1)S(1)} all-to-all(bf16[8,256,384]{1,2,0:T(8,128)(2,1)S(1)} %stack.2), channel_id=1, replica_groups=mesh['ctx'=32,'head'=8] {'head'}, dimensions={0} | all-to-all | bytes 3145728 | tf_op jit(solution)/shard_map/all_to_all | solution.py:12
  40.6 3.2 convolution_convert_fusion.3
  45.4 3.2 convolution_convert_fusion.2
  48.9 69.6 %all-gather.5.cloned.1.call-done = bf16[8192,3,128]{0,2,1:T(8,128)(2,1)} async-done(((bf16[256,3,128]{0,2,1:T(8,128)(2,1)}), bf16[8192,3,128]{0,2,1:T(8,128)(2,1)}) %all-gather.5.cloned.1.call-update) | async-done | bytes 6291472 | tf_op jit(solution)/shard_map/all_gather | solution.py:72
  118.5 8.6 %copy.27 = bf16[8192,3,128]{2,0,1:T(8,128)(2,1)} copy(bf16[8192,3,128]{0,2,1:T(8,128)(2,1)} %all-gather.5.cloned.1.call-done) | data formatting | bytes 12582912 | tf_op jit(solution)/shard_map/all_gather | solution.py:72
  127.1 71.2 %all-gather.3.cloned.1.call-done = bf16[8192,3,128]{0,2,1:T(8,128)(2,1)} async-done(((bf16[256,3,128]{0,2,1:T(8,128)(2,1)}), bf16[8192,3,128]{0,2,1:T(8,128)(2,1)}) %all-gather.3.cloned.1.call-update) | async-done | bytes 6291472 | tf_op jit(solution)/shard_map/all_gather | solution.py:71
  198.3 8.6 %copy.24 = bf16[8192,3,128]{2,0,1:T(8,128)(2,1)} copy(bf16[8192,3,128]{0,2,1:T(8,128)(2,1)} %all-gather.3.cloned.1.call-done) | data formatting | bytes 12582912 | tf_op jit(solution)/shard_map/all_gather | solution.py:71
  206.9 323.9 %while.15 = (s32[]{:T(128)}, f32[3,256]{1,0:T(4,128)S(1)}, f32[3,256]{1,0:T(4,128)S(1)}, f32[3,256,128]{2,1,0:T(8,128)S(1)}, s32[64]{0:T(128)S(1)}, /*index=5*/f...) while((s32[]{:T(128)}, f32[3,256]{1,0:T(4,128)S(1)}, ...), condition=%wide.region_3.4_spmd.clone, body=%wide.region_0.3_spmd.clone.sunk | while | flops 51515396 | bytes 2410691 | solution.py:83
  215.8 1.2 convolution_add_fusion.2
  220.8 1.2 convolution_add_fusion.2
  225.9 1.2 convolution_add_fusion.2
  236.0 1.2 convolution_add_fusion.2
  246.1 1.2 convolution_add_fusion.2
  251.2 1.2 convolution_add_fusion.2
  261.3 1.2 convolution_add_fusion.2
  266.4 1.2 convolution_add_fusion.2
  276.5 1.2 convolution_add_fusion.2
  281.6 1.2 convolution_add_fusion.2
  291.7 1.2 convolution_add_fusion.2
  301.8 1.2 convolution_add_fusion.2
  306.9 1.2 convolution_add_fusion.2
  317.0 1.2 convolution_add_fusion.2
  322.1 1.2 convolution_add_fusion.2
  332.2 1.2 convolution_add_fusion.2
  342.3 1.2 convolution_add_fusion.2
  347.4 1.2 convolution_add_fusion.2
  357.5 1.2 convolution_add_fusion.2
  362.5 1.2 convolution_add_fusion.2
  531.0 2.2 convolution_convert_fusion
  533.2 2.6 copy.33
  535.8 78.1 %reduce-scatter.4.cloned.1.call-done = bf16[384,256]{1,0:T(8,128)(2,1)} async-done(((bf16[3072,256]{1,0:T(8,128)(2,1)}), bf16[384,256]{1,0:T(8,128)(2,1)}) %reduce-scatter.4.cloned.1.call-update) | async-done | bytes 196624
  613.9 1.7 copy.34
  (525 shorter events, 178.7 us)
Async XLA Ops:
  6.5 524.5 %copy-start = (bf16[384,3072]{1,0:T(8,128)(2,1)S(1)}, bf16[384,3072]{1,0:T(8,128)(2,1)}, u32[]{:S(2)}) copy-start(bf16[384,3072]{1,0:T(8,128)(2,1)} %param.15) | copy-start | bytes 7077892
  6.5 111.9 %all-gather.5.cloned.1.call-start = ((), (), s32[]{:S(2)}) async-start(), calls=%async_computation.3 | async-start | bytes 6488064 | tf_op jit(solution)/shard_map/all_gather | solution.py:72
  7.8 30.9 %copy-start.4 = (bf16[3072,384]{1,0:T(8,128)(2,1)S(1)}, bf16[3072,384]{1,0:T(8,128)(2,1)}, u32[]{:S(2)}) copy-start(bf16[3072,384]{1,0:T(8,128)(2,1)} %param.14) | copy-start | bytes 7077892
  37.5 1.2 copy-start.1
  40.5 4.2 copy-start.2
  40.5 4.2 copy-start.3
  40.6 157.7 %all-gather.3.cloned.1.call-start = ((), (), s32[]{:S(2)}) async-start(), calls=%async_computation.2 | async-start | bytes 6488064 | tf_op jit(solution)/shard_map/all_gather | solution.py:71
  44.6 569.3 %reduce-scatter.4.cloned.1.call-start = ((), (), s32[]{:S(2)}) async-start(), calls=%async_computation.4 | async-start | bytes 1769472
Sparse Core Ops, SparseCore 0:
  40.7 77.7 all-gather.4
  120.2 77.9 all-gather.2
  535.9 77.9 reduce-scatter.3
